TPU v7x, 32 devices: a whole 2x2x4 slice. The times are simulated.
32 devices in a mesh: grp: 2 (over y), tchunk: 2 (over x), ha: 4 (over z), wa: 2 (over core).
Axes of the slice: x: 2, y: 2, z: 4, core: 2. Of those that a mesh axis runs over, the one named last changes fastest.
Arguments:
- features: bfloat16 [32, 32, 16, 192], P(('grp', 'tchunk'), 'ha', 'wa'), parts along dimension 0, may hold values from -6 to 6
- frame_counts: int32 [4], P(('grp', 'tchunk')), parts along dimension 0, may hold values from 0 to 8, as said below
- gain_first: float32 [192], replicated, may hold values from 0.25 to 1.75
- conv_first: bfloat16 [3, 3, 3, 192, 192], replicated, may hold values from -0.078125 to 0.078125
- bias_first: float32 [192], replicated, may hold values from -1.8 to 1.8
- gain_second: float32 [192], replicated, may hold values from 0.25 to 1.75
- conv_second: bfloat16 [3, 3, 3, 192, 192], replicated, may hold values from -0.078125 to 0.078125
- bias_second: float32 [192], replicated, may hold values from -1.8 to 1.8
Outputs:
- decoded: bfloat16 [32, 32, 16, 192], P(('grp', 'tchunk'), 'ha', 'wa'), parts along dimension 0
There are 2 independent parts, one for each index of `grp`. A program takes and returns all parts, laid end to end along the dimension named above; an argument that names none is the same for every part. Nothing has to cross between parts.
Inputs may be any that keep to these rules, and one draw needn't show every extreme that they name: `frame_counts`: in every draw some temporal block has all 8 slots live; any block may have none.
All inputs are finite; a program needn't handle non-finite values.
Results may differ from a plain program's by a relative error of at most 0.0039.
Values may be sent and summed in bfloat16 or wider, within the bound.
A program may use at most 64 MiB of HBM per device.

v0:
```python
import jax
import jax.numpy as jnp
from jax import lax
from jax.sharding import PartitionSpec as P

epsilon = 1e-06


def as_sent(value):

    def short(part):
        return part.astype(jnp.bfloat16) if part.dtype == jnp.float32 else part

    return jax.tree.map(short, value)


def extended(block, sides, width):
    for axis, dim in sides:
        count = lax.axis_size(axis)
        forward = [(i, i + 1) for i in range(count - 1)]
        backward = [(target, source) for source, target in forward]
        low = lax.ppermute(
            lax.slice_in_dim(block, block.shape[dim] - width, None, axis=dim), axis, forward
        )
        high = lax.ppermute(lax.slice_in_dim(block, 0, width, axis=dim), axis, backward)
        block = jnp.concatenate([low, block, high], axis=dim)
    return block


def prefix(value, axis, combine, identity):
    devices, position = (lax.axis_size(axis), lax.axis_index(axis))
    everything = jax.tree.map(lambda part: lax.all_gather(part, axis), value)
    start = jax.tree.map(
        lambda part, zero: jnp.broadcast_to(jnp.asarray(zero, part.dtype), part.shape),
        value,
        identity,
    )

    def turn(k, before):
        reached = k < position
        new = combine(before, jax.tree.map(lambda part: part[k], everything))
        return jax.tree.map(lambda a, b: jnp.where(reached, a, b), new, before)

    return lax.fori_loop(0, devices, turn, start)


def activate(values, gain):
    values = values.astype(jnp.float32)
    inverse = lax.rsqrt(jnp.mean(values * values, axis=-1, keepdims=True) + epsilon)
    return jax.nn.silu(values * inverse * gain).astype(jnp.bfloat16)


def causal_conv(stacked, kernel, bias_term):
    result = lax.conv_general_dilated(
        stacked[None],
        kernel,
        (1, 1, 1),
        "VALID",
        dimension_numbers=("NDHWC", "DHWIO", "NDHWC"),
        preferred_element_type=jnp.float32,
    )
    return result[0] + bias_term


def bordered_conv(stacked, kernel, bias_term):
    padded = extended(as_sent(stacked), (("ha", 1), ("wa", 2)), 1).astype(stacked.dtype)
    return causal_conv(padded, kernel, bias_term)


def own_tail(inputs, frame_total):
    padded = jnp.concatenate([jnp.zeros((2,) + inputs.shape[1:], inputs.dtype), inputs], axis=0)
    return lax.dynamic_slice_in_dim(padded, frame_total, 2, 0)


def join_tails(earlier, latest):
    early_frames, early_total = earlier
    late_frames, late_total = latest
    moved = jnp.concatenate([early_frames[1:], late_frames[1:]], axis=0)
    frames = jnp.where(
        late_total[0] >= 2, late_frames, jnp.where(late_total[0] >= 1, moved, early_frames)
    )
    return (frames, jnp.minimum(early_total + late_total, 2))


def receive_cache(tail_frames, tail_total):
    empty = (jnp.zeros_like(tail_frames), jnp.zeros_like(tail_total))
    return prefix((tail_frames, tail_total), "tchunk", join_tails, empty)[0]


def shards(
    features,
    frame_counts,
    gain_first,
    conv_first,
    bias_first,
    gain_second,
    conv_second,
    bias_second,
):
    frames_here = features.shape[0]
    frame_total = frame_counts[0]
    total_word = frame_counts.astype(jnp.bfloat16)
    valid_mask = (jnp.arange(frames_here) < frame_total)[:, None, None, None]
    first_input = jnp.where(valid_mask, activate(features, gain_first), jnp.zeros((), jnp.bfloat16))
    first_cache = receive_cache(own_tail(first_input, frame_total), total_word)
    first_joined = jnp.concatenate([first_cache, first_input], axis=0)
    hidden = bordered_conv(first_joined, conv_first, bias_first)
    second_input = jnp.where(valid_mask, activate(hidden, gain_second), jnp.zeros((), jnp.bfloat16))
    second_cache = receive_cache(own_tail(second_input, frame_total), total_word)
    result = bordered_conv(
        jnp.concatenate([second_cache, second_input], axis=0), conv_second, bias_second
    )
    decoded = jnp.where(
        valid_mask, features.astype(jnp.float32) + result, jnp.zeros((), jnp.float32)
    )
    return decoded.astype(jnp.bfloat16)


def solution(mesh):
    return jax.shard_map(
        shards,
        mesh=mesh,
        in_specs=(
            P(("grp", "tchunk"), "ha", "wa", None),
            P(("grp", "tchunk")),
            P(),
            P(),
            P(),
            P(),
            P(),
            P(),
        ),
        out_specs=P(("grp", "tchunk"), "ha", "wa", None),
        check_vma=False,
    )
```

profile of v0, /device:TPU:0, one launch (start us, length us, event | category | flops | bytes accessed | tf_op | source)
XLA Modules:
  0.0 77.5 jit_solution(14101113584248772910)
XLA Ops:
  0.0 0.0 copy-start
  0.8 1.1 %fusion.8 = f32[8,8,8]{2,1,0:T(8,128)S(1)} fusion(bf16[8,8,8,192]{3,2,1,0:T(8,128)(2,1)} %param.12), kind=kLoop, calls=%fused_computation.21 | loop fusion | flops 294400 | bytes 198656 | tf_op jit(solution)/shard_map/reduce_sum | solution.py:49
  2.0 1.2 %fusion.18 = bf16[8,8,8,192]{3,2,1,0:T(8,128)(2,1)S(1)} fusion(bf16[8,8,8,192]{3,2,1,0:T(8,128)(2,1)} %param.12, f32[192]{0:T(256)} %param.14, f32[8,8,8]{2,1,0:T(8,128)S(1)} %add_rsqrt_fusion.1, pred[8]{0:T(512)(128)(4,1)S(1)} %iota_compare_fusion), kind=kLoop, calls=%fused_computation.37 | loop fusion | flops 884736 | bytes 396040 | tf_op jit(solution)/shard_map/jit(_where)/select_n | solution.py:104
  3.2 5.9 %all-gather.1 = bf16[4,8,8,192]{3,2,1,0:T(8,128)(2,1)S(1)} all-gather(bf16[2,8,8,192]{3,2,1,0:T(8,128)(2,1)S(1)} %pad_dynamic-slice_fusion.1), channel_id=3, replica_groups=mesh['grp'=2,'tchunk'=2,'ha'=4,'wa'=2] {'tchunk'}, dimensions={0}, use_global_device_ids=true | all-gather | bytes 147456 | tf_op jit(solution)/shard_map/all_gather | solution.py:32
  9.1 1.2 %dynamic-slice = u32[1]{0:T(128)} dynamic-slice(u32[32]{0:T(128)} %constant.104, u32[]{:T(128)S(6)} %add.104), dynamic_slice_sizes={1} | dynamic-slice | bytes 12
  10.3 0.8 dynamic-update-slice
  11.1 4.9 %all-reduce.2 = bf16[2]{0:T(256)(128)(2,1)S(1)} all-reduce(bf16[2]{0:T(256)(128)(2,1)S(1)} %dynamic-update-slice), channel_id=2, replica_groups=mesh['grp'=2,'tchunk'=2,'ha'=4,'wa'=2] {'tchunk'}, use_global_device_ids=true, to_apply=%add.2 | all-reduce | flops 2 | bytes 8
  16.0 0.1 copy.18
  16.1 3.7 %while.28 = (s32[]{:T(128)}, bf16[2,8,8,192]{3,2,1,0:T(8,128)(2,1)S(1)}, s32[]{:T(128)}, bf16[2,1]{1,0:T(2,128)(2,1)S(1)}, bf16[2,2,8,8,192]{4,3,2,1,0:T(8,128)(...) while((s32[]{:T(128)}, bf16[2,8,8,192]{3,2,1,0:T(8,128)(2,1)S(1)}, s32[]{:T(128)}, ...), condition=%wide.region_2.3_spmd.clone, body=%wide.region_1.2_spmd.clone.sunk | while | flops 147465 | bytes 393370 | solution.py:44
  16.1 0.6 fusion.27
  17.3 0.6 fusion.28
  18.0 0.6 fusion.27
  19.2 0.6 fusion.28
  19.9 4.0 %collective-permute-start = (bf16[10,1,8,192]{3,2,1,0:T(8,128)(2,1)S(1)}, bf16[10,1,8,192]{3,2,1,0:T(8,128)(2,1)S(1)}, u32[]{:S(2)}, u32[]{:S(2)}) collective-permute-start(bf16[10,1,8,192]{3,2,1,0:T(8,128)(2,1)S(1)} %get-tuple-element.291), channel_id=1, source_target_pairs={{0,2},{2,4},{4,6},{1,3},{3,5},{5,7},{8,10},{10,12},{12,14},{9,11},... | collective-permute-start | bytes 92168 | tf_op jit(solution)/shard_map/ppermute | solution.py:22
  23.9 1.3 %collective-permute-start.1 = (bf16[10,1,8,192]{3,2,1,0:T(8,128)(2,1)S(1)}, bf16[10,1,8,192]{3,2,1,0:T(8,128)(2,1)S(1)}, u32[]{:S(2)}, u32[]{:S(2)}) collective-permute-start(bf16[10,1,8,192]{3,2,1,0:T(8,128)(2,1)S(1)} %get-tuple-element.292), channel_id=1, source_target_pairs={{2,0},{4,2},{6,4},{3,1},{5,3},{7,5},{10,8},{12,10},{14,12},{11,9},... | collective-permute-start | bytes 92168 | tf_op jit(solution)/shard_map/ppermute | solution.py:25
  25.2 0.4 collective-permute-done
  25.5 4.2 %collective-permute-done.1 = bf16[10,1,8,192]{3,2,1,0:T(8,128)(2,1)S(1)} collective-permute-done((bf16[10,1,8,192]{3,2,1,0:T(8,128)(2,1)S(1)}, bf16[10,1,8,192]{3,2,1,0:T(8,128)(2,1)S(1)}, u32[]{:S(2)}, u32[]{:S(2)}) %collective-permute-start.1) | collective-permute-done | bytes 30752 | tf_op jit(solution)/shard_map/ppermute | solution.py:25
  29.8 0.2 pad_maximum_fusion.7
  29.9 1.3 %collective-permute-start.2 = (bf16[10,10,1,192]{3,2,1,0:T(2,128)(2,1)S(1)}, bf16[10,10,1,192]{3,2,1,0:T(2,128)(2,1)S(1)}, u32[]{:S(2)}, u32[]{:S(2)}) collective-permute-start(bf16[10,10,1,192]{3,2,1,0:T(2,128)(2,1)S(1)} %get-tuple-element.287), channel_id=1, source_target_pairs={{0,1},{2,3},{4,5},{6,7},{8,9},{10,11},{12,13},{14,15},{16,17},{18,... | collective-permute-start | bytes 115208 | tf_op jit(solution)/shard_map/ppermute | solution.py:22
  31.2 1.3 %collective-permute-start.3 = (bf16[10,10,1,192]{3,2,1,0:T(2,128)(2,1)S(1)}, bf16[10,10,1,192]{3,2,1,0:T(2,128)(2,1)S(1)}, u32[]{:S(2)}, u32[]{:S(2)}) collective-permute-start(bf16[10,10,1,192]{3,2,1,0:T(2,128)(2,1)S(1)} %get-tuple-element.288), channel_id=1, source_target_pairs={{1,0},{3,2},{5,4},{7,6},{9,8},{11,10},{13,12},{15,14},{17,16},{19,... | collective-permute-start | bytes 115208 | tf_op jit(solution)/shard_map/ppermute | solution.py:25
  32.6 0.0 collective-permute-done.2
  32.6 1.9 %collective-permute-done.3 = bf16[10,10,1,192]{3,2,1,0:T(2,128)(2,1)S(1)} collective-permute-done((bf16[10,10,1,192]{3,2,1,0:T(2,128)(2,1)S(1)}, bf16[10,10,1,192]{3,2,1,0:T(2,128)(2,1)S(1)}, u32[]{:S(2)}, u32[]{:S(2)}) %collective-permute-start.3) | collective-permute-done | bytes 38432 | tf_op jit(solution)/shard_map/ppermute | solution.py:25
  34.4 0.5 maximum_bitcast_fusion
  35.0 0.0 copy-done
  35.0 0.0 copy-start.2
  35.0 0.0 copy-start.3
  35.0 8.1 %fusion.6 = f32[1,8,8,8,192]{4,0,3,2,1:T(1,128)S(1)} fusion(bf16[3,3,3,192,192]{4,3,2,1,0:T(8,128)(2,1)S(1)} %copy-done, bf16[1,10,10,10,192]{4,3,2,1,0:T(8,128)(2,1)S(1)} %maximum_bitcast_fusion), kind=kOutput, calls=%fused_computation.14 | convolution fusion | flops 1019215872 | bytes 2767872 | tf_op jit(solution)/shard_map/conv_general_dilated | solution.py:54
  43.1 0.0 copy-done.2
  43.1 0.1 multiply_reduce_fusion
  43.2 0.0 copy-done.3
  43.2 0.2 broadcast_select_fusion.2
  43.5 4.9 %all-gather.2 = bf16[4,8,8,192]{3,2,1,0:T(8,128)(2,1)S(1)} all-gather(bf16[2,8,8,192]{3,2,1,0:T(8,128)(2,1)S(1)} %pad_dynamic-slice_fusion), channel_id=4, replica_groups=mesh['grp'=2,'tchunk'=2,'ha'=4,'wa'=2] {'tchunk'}, dimensions={0}, use_global_device_ids=true | all-gather | bytes 147456 | tf_op jit(solution)/shard_map/all_gather | solution.py:32
  48.5 3.7 %while.29 = (s32[]{:T(128)}, bf16[2,8,8,192]{3,2,1,0:T(8,128)(2,1)S(1)}, s32[]{:T(128)}, bf16[2,1]{1,0:T(2,128)(2,1)S(1)}, bf16[2,2,8,8,192]{4,3,2,1,0:T(8,128)(...) while((s32[]{:T(128)}, bf16[2,8,8,192]{3,2,1,0:T(8,128)(2,1)S(1)}, s32[]{:T(128)}, ...), condition=%wide.region_5.6_spmd.clone, body=%wide.region_4.5_spmd.clone.sunk | while | flops 147465 | bytes 393370 | solution.py:44
  48.5 0.6 fusion.29
  49.7 0.6 fusion.30
  50.3 0.6 fusion.29
  51.6 0.6 fusion.30
  52.2 3.5 %collective-permute-start.4 = (bf16[10,1,8,192]{3,2,1,0:T(8,128)(2,1)S(1)}, bf16[10,1,8,192]{3,2,1,0:T(8,128)(2,1)S(1)}, u32[]{:S(2)}, u32[]{:S(2)}) collective-permute-start(bf16[10,1,8,192]{3,2,1,0:T(8,128)(2,1)S(1)} %get-tuple-element.289), channel_id=1, source_target_pairs={{0,2},{2,4},{4,6},{1,3},{3,5},{5,7},{8,10},{10,12},{12,14},{9,11},... | collective-permute-start | bytes 92168 | tf_op jit(solution)/shard_map/ppermute | solution.py:22
  55.7 1.3 %collective-permute-start.5 = (bf16[10,1,8,192]{3,2,1,0:T(8,128)(2,1)S(1)}, bf16[10,1,8,192]{3,2,1,0:T(8,128)(2,1)S(1)}, u32[]{:S(2)}, u32[]{:S(2)}) collective-permute-start(bf16[10,1,8,192]{3,2,1,0:T(8,128)(2,1)S(1)} %get-tuple-element.290), channel_id=1, source_target_pairs={{2,0},{4,2},{6,4},{3,1},{5,3},{7,5},{10,8},{12,10},{14,12},{11,9},... | collective-permute-start | bytes 92168 | tf_op jit(solution)/shard_map/ppermute | solution.py:25
  57.0 0.4 collective-permute-done.4
  57.4 4.2 %collective-permute-done.5 = bf16[10,1,8,192]{3,2,1,0:T(8,128)(2,1)S(1)} collective-permute-done((bf16[10,1,8,192]{3,2,1,0:T(8,128)(2,1)S(1)}, bf16[10,1,8,192]{3,2,1,0:T(8,128)(2,1)S(1)}, u32[]{:S(2)}, u32[]{:S(2)}) %collective-permute-start.5) | collective-permute-done | bytes 30752 | tf_op jit(solution)/shard_map/ppermute | solution.py:25
  61.6 0.2 pad_maximum_fusion.3
  61.8 1.3 %collective-permute-start.6 = (bf16[10,10,1,192]{3,2,1,0:T(2,128)(2,1)S(1)}, bf16[10,10,1,192]{3,2,1,0:T(2,128)(2,1)S(1)}, u32[]{:S(2)}, u32[]{:S(2)}) collective-permute-start(bf16[10,10,1,192]{3,2,1,0:T(2,128)(2,1)S(1)} %get-tuple-element.285), channel_id=1, source_target_pairs={{0,1},{2,3},{4,5},{6,7},{8,9},{10,11},{12,13},{14,15},{16,17},{18,... | collective-permute-start | bytes 115208 | tf_op jit(solution)/shard_map/ppermute | solution.py:22
  63.1 1.5 %collective-permute-start.7 = (bf16[10,10,1,192]{3,2,1,0:T(2,128)(2,1)S(1)}, bf16[10,10,1,192]{3,2,1,0:T(2,128)(2,1)S(1)}, u32[]{:S(2)}, u32[]{:S(2)}) collective-permute-start(bf16[10,10,1,192]{3,2,1,0:T(2,128)(2,1)S(1)} %get-tuple-element.286), channel_id=1, source_target_pairs={{1,0},{3,2},{5,4},{7,6},{9,8},{11,10},{13,12},{15,14},{17,16},{19,... | collective-permute-start | bytes 115208 | tf_op jit(solution)/shard_map/ppermute | solution.py:25
  64.6 0.0 collective-permute-done.6
  64.6 1.7 %collective-permute-done.7 = bf16[10,10,1,192]{3,2,1,0:T(2,128)(2,1)S(1)} collective-permute-done((bf16[10,10,1,192]{3,2,1,0:T(2,128)(2,1)S(1)}, bf16[10,10,1,192]{3,2,1,0:T(2,128)(2,1)S(1)}, u32[]{:S(2)}, u32[]{:S(2)}) %collective-permute-start.7) | collective-permute-done | bytes 38432 | tf_op jit(solution)/shard_map/ppermute | solution.py:25
  66.3 0.5 maximum_bitcast_fusion.1
  66.8 0.0 copy-start.1
  66.8 0.0 copy-start.4
  66.8 9.8 %fusion.4 = f32[1,8,8,8,192]{4,0,3,2,1:T(1,128)S(1)} fusion(bf16[3,3,3,192,192]{4,3,2,1,0:T(8,128)(2,1)} %param.18, bf16[1,10,10,10,192]{4,3,2,1,0:T(8,128)(2,1)S(1)} %maximum_bitcast_fusion.1), kind=kOutput, calls=%fused_computation.12 | convolution fusion | flops 1019215872 | bytes 2767872 | tf_op jit(solution)/shard_map/conv_general_dilated | solution.py:54
  76.7 0.0 copy-done.1
  76.7 0.0 copy-done.4
  76.7 0.8 %fusion.17 = bf16[8,8,8,192]{3,2,1,0:T(8,128)(2,1)} fusion(bf16[8,8,8,192]{3,2,1,0:T(8,128)(2,1)S(1)} %copy-done.1, f32[1,8,8,8,192]{4,0,3,2,1:T(1,128)S(1)} %fusion.4, f32[192]{0:T(256)S(1)} %copy-done.4, pred[8]{0:T(512)(128)(4,1)S(1)} %iota_compare_fusion), kind=kLoop, calls=%fused_computation.30 | loop fusion | flops 491520 | bytes 787208 | tf_op jit(solution)/shard_map/convert_element_type | solution.py:116
  (22 shorter events, 0.2 us)
Async XLA Ops:
  0.0 35.0 %copy-start = (bf16[3,3,3,192,192]{4,3,2,1,0:T(8,128)(2,1)S(1)}, bf16[3,3,3,192,192]{4,3,2,1,0:T(8,128)(2,1)}, u32[]{:S(2)}) copy-start(bf16[3,3,3,192,192]{4,3,2,1,0:T(8,128)(2,1)} %param.15) | copy-start | bytes 5971972
  19.9 5.7 %collective-permute-start = (bf16[10,1,8,192]{3,2,1,0:T(8,128)(2,1)S(1)}, bf16[10,1,8,192]{3,2,1,0:T(8,128)(2,1)S(1)}, u32[]{:S(2)}, u32[]{:S(2)}) collective-permute-start(bf16[10,1,8,192]{3,2,1,0:T(8,128)(2,1)S(1)} %get-tuple-element.291), channel_id=1, source_target_pairs={{0,2},{2,4},{4,6},{1,3},{3,5},{5,7},{8,10},{10,12},{12,14},{9,11},... | collective-permute-start | bytes 92168 | tf_op jit(solution)/shard_map/ppermute | solution.py:22
  23.9 5.9 %collective-permute-start.1 = (bf16[10,1,8,192]{3,2,1,0:T(8,128)(2,1)S(1)}, bf16[10,1,8,192]{3,2,1,0:T(8,128)(2,1)S(1)}, u32[]{:S(2)}, u32[]{:S(2)}) collective-permute-start(bf16[10,1,8,192]{3,2,1,0:T(8,128)(2,1)S(1)} %get-tuple-element.292), channel_id=1, source_target_pairs={{2,0},{4,2},{6,4},{3,1},{5,3},{7,5},{10,8},{12,10},{14,12},{11,9},... | collective-permute-start | bytes 92168 | tf_op jit(solution)/shard_map/ppermute | solution.py:25
  29.9 2.6 %collective-permute-start.2 = (bf16[10,10,1,192]{3,2,1,0:T(2,128)(2,1)S(1)}, bf16[10,10,1,192]{3,2,1,0:T(2,128)(2,1)S(1)}, u32[]{:S(2)}, u32[]{:S(2)}) collective-permute-start(bf16[10,10,1,192]{3,2,1,0:T(2,128)(2,1)S(1)} %get-tuple-element.287), channel_id=1, source_target_pairs={{0,1},{2,3},{4,5},{6,7},{8,9},{10,11},{12,13},{14,15},{16,17},{18,... | collective-permute-start | bytes 115208 | tf_op jit(solution)/shard_map/ppermute | solution.py:22
  31.2 3.2 %collective-permute-start.3 = (bf16[10,10,1,192]{3,2,1,0:T(2,128)(2,1)S(1)}, bf16[10,10,1,192]{3,2,1,0:T(2,128)(2,1)S(1)}, u32[]{:S(2)}, u32[]{:S(2)}) collective-permute-start(bf16[10,10,1,192]{3,2,1,0:T(2,128)(2,1)S(1)} %get-tuple-element.288), channel_id=1, source_target_pairs={{1,0},{3,2},{5,4},{7,6},{9,8},{11,10},{13,12},{15,14},{17,16},{19,... | collective-permute-start | bytes 115208 | tf_op jit(solution)/shard_map/ppermute | solution.py:25
  35.0 8.1 %copy-start.2 = (f32[192]{0:T(256)S(1)}, f32[192]{0:T(256)}, u32[]{:S(2)}) copy-start(f32[192]{0:T(256)} %param.16) | copy-start | bytes 2308
  35.0 8.3 %copy-start.3 = (f32[192]{0:T(256)S(1)}, f32[192]{0:T(256)}, u32[]{:S(2)}) copy-start(f32[192]{0:T(256)} %param.17) | copy-start | bytes 2308
  52.2 5.1 %collective-permute-start.4 = (bf16[10,1,8,192]{3,2,1,0:T(8,128)(2,1)S(1)}, bf16[10,1,8,192]{3,2,1,0:T(8,128)(2,1)S(1)}, u32[]{:S(2)}, u32[]{:S(2)}) collective-permute-start(bf16[10,1,8,192]{3,2,1,0:T(8,128)(2,1)S(1)} %get-tuple-element.289), channel_id=1, source_target_pairs={{0,2},{2,4},{4,6},{1,3},{3,5},{5,7},{8,10},{10,12},{12,14},{9,11},... | collective-permute-start | bytes 92168 | tf_op jit(solution)/shard_map/ppermute | solution.py:22
  55.7 5.9 %collective-permute-start.5 = (bf16[10,1,8,192]{3,2,1,0:T(8,128)(2,1)S(1)}, bf16[10,1,8,192]{3,2,1,0:T(8,128)(2,1)S(1)}, u32[]{:S(2)}, u32[]{:S(2)}) collective-permute-start(bf16[10,1,8,192]{3,2,1,0:T(8,128)(2,1)S(1)} %get-tuple-element.290), channel_id=1, source_target_pairs={{2,0},{4,2},{6,4},{3,1},{5,3},{7,5},{10,8},{12,10},{14,12},{11,9},... | collective-permute-start | bytes 92168 | tf_op jit(solution)/shard_map/ppermute | solution.py:25
  61.8 2.8 %collective-permute-start.6 = (bf16[10,10,1,192]{3,2,1,0:T(2,128)(2,1)S(1)}, bf16[10,10,1,192]{3,2,1,0:T(2,128)(2,1)S(1)}, u32[]{:S(2)}, u32[]{:S(2)}) collective-permute-start(bf16[10,10,1,192]{3,2,1,0:T(2,128)(2,1)S(1)} %get-tuple-element.285), channel_id=1, source_target_pairs={{0,1},{2,3},{4,5},{6,7},{8,9},{10,11},{12,13},{14,15},{16,17},{18,... | collective-permute-start | bytes 115208 | tf_op jit(solution)/shard_map/ppermute | solution.py:22
  63.1 3.2 %collective-permute-start.7 = (bf16[10,10,1,192]{3,2,1,0:T(2,128)(2,1)S(1)}, bf16[10,10,1,192]{3,2,1,0:T(2,128)(2,1)S(1)}, u32[]{:S(2)}, u32[]{:S(2)}) collective-permute-start(bf16[10,10,1,192]{3,2,1,0:T(2,128)(2,1)S(1)} %get-tuple-element.286), channel_id=1, source_target_pairs={{1,0},{3,2},{5,4},{7,6},{9,8},{11,10},{13,12},{15,14},{17,16},{19,... | collective-permute-start | bytes 115208 | tf_op jit(solution)/shard_map/ppermute | solution.py:25
  66.8 9.9 %copy-start.1 = (bf16[8,8,8,192]{3,2,1,0:T(8,128)(2,1)S(1)}, bf16[8,8,8,192]{3,2,1,0:T(8,128)(2,1)}, u32[]{:S(2)}) copy-start(bf16[8,8,8,192]{3,2,1,0:T(8,128)(2,1)} %param.12) | copy-start | bytes 589828
  66.8 9.9 %copy-start.4 = (f32[192]{0:T(256)S(1)}, f32[192]{0:T(256)}, u32[]{:S(2)}) copy-start(f32[192]{0:T(256)} %param.19) | copy-start | bytes 2308
where the time goes:
time: 78 us; the launch traced here: 77.5 us
  matrix products  17.9 us (23%)
  blocking collectives  15.7 us (20%)
  starting transfers between devices  15.4 us (20%)
  waiting for transfers between devices  12.8 us (16%)
  other arithmetic  9.52 us (12%)
  loops' own time  2.76 us (4%)
  local copies, waits for them, and re-layouts  2.27 us (3%)
  between operations  1.11 us (1%)
    conv_general_dilated x2, matrix products, causal_conv(): lax.conv_general_dilated(stacked[None], kernel, (1, 1, 1), 'VALID', dimen...  17.9 us
    ppermute x4, waiting for transfers between devices, extended(): lax.ppermute(lax.slice_in_dim(block, 0, width, axis=dim), axis, backward)  12.1 us
    all_gather x2, blocking collectives, prefix(): everything = jax.tree.map(lambda part: lax.all_gather(part, axis), value)  10.8 us
    ppermute x4, starting transfers between devices, extended(): lax.ppermute(lax.slice_in_dim(block, block.shape[dim] - width, None, axis...  10.1 us
    ppermute x4, starting transfers between devices, extended(): lax.ppermute(lax.slice_in_dim(block, 0, width, axis=dim), axis, backward)  5.35 us
    unnamed x1, blocking collectives  4.92 us
    another operation x2, loops' own time, prefix(): return lax.fori_loop(0, devices, turn, start)  2.76 us
    select_n x4, other arithmetic, turn(): return jax.tree.map(lambda a, b: jnp.where(reached, a, b), new, before)  2.38 us
  transfers between devices with their start and end apart: 8, of which 6 were waited for; matrix products, arithmetic and copies ran while one was open for 0% of the time, Pallas kernels for 0%

commit v1 on v0

v1 whole, which is shorter than its diff:
```python
import functools

import jax
import jax.numpy as jnp
from jax import lax
from jax.experimental import pallas as pl
from jax.experimental.pallas import tpu as pltpu
from jax.sharding import PartitionSpec as P

epsilon = 1e-06
MESH = pl.DeviceIdType.MESH
DIRS = [(dz, dw) for dz in (-1, 0, 1) for dw in (-1, 0, 1)]
f32, bf16 = jnp.float32, jnp.bfloat16


def silu_norm(values, gain):
    inverse = lax.rsqrt(jnp.mean(values * values, axis=-1, keepdims=True) + epsilon)
    return jax.nn.silu(values * inverse * gain)


def both(*conds):
    out = conds[0]
    for c in conds[1:]:
        out = jnp.logical_and(out, c)
    return out


def kernel(sizes, *refs):
    placed, out, scratch = refs[:8], refs[8], refs[9:]
    n_t, n_z, n_w = sizes
    (cnt_ref, feat, g1, w1, b1, g2, w2, b2) = local = scratch[:8]
    frames, rows, cols, chans = feat.shape
    (lsem, even, odd, acc, cnt_own, cnt_in, carry, carry_col, csend, crecv) = scratch[8:18]
    phases = (scratch[18:30], scratch[30:42])
    me_t, me_z, me_w = lax.axis_index("tchunk"), lax.axis_index("ha"), lax.axis_index("wa")
    loads = [pltpu.make_async_copy(src, dst, lsem.at[i]) for i, (src, dst) in enumerate(zip(placed, local))]
    for i in (1, 2, 4, 5, 7, 3, 6):
        loads[i].start()

    def exists(dz, dw):
        z, w = me_z + dz, me_w + dw
        return both(z >= 0, z < n_z, w >= 0, w < n_w)

    def device(k, dz, dw):
        return {"tchunk": k, "ha": lax.rem(me_z + dz + n_z, n_z), "wa": lax.rem(me_w + dw + n_w, n_w)}

    barrier = pltpu.get_barrier_semaphore()
    expected = jnp.int32(0)
    for k in range(n_t):
        for dz, dw in DIRS:
            there = exists(dz, dw)
            if (dz, dw) == (0, 0):
                there = me_t != k
            expected = expected + there.astype(jnp.int32)

            @pl.when(there)
            def _(k=k, dz=dz, dw=dw):
                pl.semaphore_signal(barrier, inc=1, device_id=device(k, dz, dw), device_id_type=MESH)

    x_of = lax.broadcasted_iota(jnp.int32, (frames, cols, chans), 1)
    t_of = lax.broadcasted_iota(jnp.int32, (frames, cols, chans), 0)
    def near(bufs, dz, dw):
        own, own_col, _, _, row_in, col_in = bufs[:6]
        y, yy = (0, rows + 1) if dz < 0 else (rows - 1, 0)
        s, ss = (0, 1) if dw < 0 else (1, 0)
        if dw == 0:
            return own.at[y, pl.ds(2, frames)], row_in.at[1 if dz < 0 else 0]
        if dz == 0:
            return own_col.at[s], col_in.at[ss, pl.ds(1, rows)]
        return own_col.at[s, y], col_in.at[ss, yy]

    def far(bufs, slot, dz, dw):
        tail, tail_col, tail_in, tailc_in = bufs[2], bufs[3], bufs[6], bufs[7]
        s, ss = (0, 1) if dw < 0 else (1, 0)
        if dw == 0:
            if dz == 0:
                return tail, tail_in.at[slot, pl.ds(1, rows)]
            y, yy = (0, rows + 1) if dz < 0 else (rows - 1, 0)
            return tail.at[y], tail_in.at[slot, yy]
        return tail_col.at[s], tailc_in.at[slot, ss, 1 - dz]

    def near_copy(bufs, dz, dw, way=1):
        src, dst = near(bufs, dz, dw)
        i = DIRS.index((dz, dw))
        return pltpu.make_async_remote_copy(
            src, dst, bufs[8].at[i], bufs[9].at[i], device_id=device(me_t, way * dz, way * dw), device_id_type=MESH
        )

    def far_copy(bufs, k, slot, dz, dw, way=1):
        src, dst = far(bufs, slot, dz, dw)
        i = DIRS.index((dz, dw))
        return pltpu.make_async_remote_copy(
            src, dst, bufs[10].at[k, i], bufs[11].at[slot, i],
            device_id=device(k, way * dz, way * dw), device_id_type=MESH,
        )

    def count_copy(k, slot):
        return pltpu.make_async_remote_copy(
            cnt_own, cnt_in.at[slot], csend.at[k], crecv.at[slot],
            device_id=device(k, 0, 0), device_id_type=MESH,
        )

    def clear(bufs):
        bufs[0][:, :2] = jnp.zeros((rows, 2, cols, chans), bf16)
        for dz, dw in DIRS:
            if (dz, dw) == (0, 0):
                continue

            @pl.when(jnp.logical_not(exists(-dz, -dw)))
            def _(dz=dz, dw=dw):
                dst = near(bufs, dz, dw)[1]
                dst[...] = jnp.zeros(dst.shape, dst.dtype)
                for k in range(n_t):
                    dst = far(bufs, k, dz, dw)[1]
                    dst[...] = jnp.zeros(dst.shape, dst.dtype)

    def keep(bufs, y, value):
        own, own_col = bufs[0], bufs[1]
        value = jnp.where(live, value, 0.0)
        own[y, 2:] = value.astype(bf16)
        own_col[0, y] = value[:, 0, :].astype(bf16)
        own_col[1, y] = value[:, cols - 1, :].astype(bf16)

    def keep_tail(bufs):
        own, _, tail, tail_col = bufs[:4]
        for f in range(2):
            frame = own[:, count + f].astype(f32)
            tail[:, f] = frame.astype(bf16)
            tail_col[0, f] = frame[:, 0, :].astype(bf16)
            tail_col[1, f] = frame[:, cols - 1, :].astype(bf16)

    def send(bufs, first):
        for k in range(1, n_t):
            @pl.when(me_t < k)
            def _(k=k):
                if first:
                    count_copy(k, me_t).start()
                for dz, dw in DIRS:
                    @pl.when(exists(dz, dw))
                    def _(dz=dz, dw=dw):
                        far_copy(bufs, k, me_t, dz, dw).start()
        for dz, dw in DIRS:
            if (dz, dw) != (0, 0):
                @pl.when(exists(dz, dw))
                def _(dz=dz, dw=dw):
                    near_copy(bufs, dz, dw).start()

    def receive_near(bufs):
        for dz, dw in DIRS:
            if (dz, dw) != (0, 0):
                @pl.when(exists(-dz, -dw))
                def _(dz=dz, dw=dw):
                    near_copy(bufs, dz, dw, -1).wait_recv()

    def receive_far(bufs, first):
        tail_in, tailc_in = bufs[6], bufs[7]
        carry[...] = jnp.zeros(carry.shape, f32)
        carry_col[...] = jnp.zeros(carry_col.shape, f32)
        for k in range(n_t - 1):
            @pl.when(me_t > k)
            def _(k=k):
                if first:
                    count_copy(k, k).wait_recv()
                for dz, dw in DIRS:
                    @pl.when(exists(-dz, -dw))
                    def _(dz=dz, dw=dw):
                        far_copy(bufs, k, k, dz, dw, -1).wait_recv()
                total = cnt_in[k]
                two, one = total > 1.5, total > 0.5

                def merge(ref, index, late0, late1):
                    early0, early1 = ref[index + (0,)], ref[index + (1,)]
                    ref[index + (0,)] = jnp.where(two, late0, jnp.where(one, early1, early0))
                    ref[index + (1,)] = jnp.where(one, late1, early1)

                for yy in range(rows + 2):
                    merge(carry, (yy,), tail_in[k, yy, 0].astype(f32), tail_in[k, yy, 1].astype(f32))
                for s in range(2):
                    for d in range(3):
                        merge(carry_col, (s, d), tailc_in[k, s, d, 0].astype(f32), tailc_in[k, s, d, 1].astype(f32))

    def finish_sends(bufs, first):
        for k in range(1, n_t):
            @pl.when(me_t < k)
            def _(k=k):
                if first:
                    count_copy(k, me_t).wait_send()
                for dz, dw in DIRS:
                    @pl.when(exists(dz, dw))
                    def _(dz=dz, dw=dw):
                        far_copy(bufs, k, me_t, dz, dw).wait_send()
        for dz, dw in DIRS:
            if (dz, dw) != (0, 0):
                @pl.when(exists(dz, dw))
                def _(dz=dz, dw=dw):
                    near_copy(bufs, dz, dw).wait_send()

    def spread(block, col_left, col_right):
        count_t = block.shape[0]
        flat = block.reshape(count_t * cols, chans)
        xi = lax.broadcasted_iota(jnp.int32, block.shape, 1)
        left = pltpu.roll(flat, 1, 0).reshape(block.shape)
        left = jnp.where(xi == 0, jnp.broadcast_to(col_left[:, None, :], block.shape), left)
        right = pltpu.roll(flat, count_t * cols - 1, 0).reshape(block.shape)
        right = jnp.where(xi == cols - 1, jnp.broadcast_to(col_right[:, None, :], block.shape), right)
        return jnp.concatenate(
            [left.reshape(flat.shape), flat, right.reshape(flat.shape)], axis=1
        )

    def place(bufs, yy, block):
        col_in = bufs[5]
        got = spread(block, col_in[0, yy].astype(f32), col_in[1, yy].astype(f32))
        even[yy, 2 * cols :] = got.astype(bf16)
        odd[yy, cols : 2 * cols] = got[:cols].astype(bf16)
        odd[yy, 2 * cols :] = got[cols : (frames - 1) * cols].astype(bf16)

    def place_carry(yy):
        d, at = (0, rows - 1) if yy == 0 else (2, 0) if yy == rows + 1 else (1, yy - 1)
        left = carry_col[0, d, :, pl.ds(at, 1), :].reshape(2, chans)
        right = carry_col[1, d, :, pl.ds(at, 1), :].reshape(2, chans)
        got = spread(carry[yy], left, right)
        even[yy, : 2 * cols] = got.astype(bf16)
        odd[yy, :cols] = got[cols:].astype(bf16)

    def gather(bufs, first):
        own, row_in = bufs[0], bufs[4]
        receive_near(bufs)

        for y in range(rows):
            place(bufs, y + 1, own[y, 2:].astype(f32))

        place(bufs, 0, row_in[0].astype(f32))
        place(bufs, rows + 1, row_in[1].astype(f32))
        receive_far(bufs, first)
        for yy in range(rows + 2):
            place_carry(yy)

    def conv(weights):
        size = frames * cols
        for a in range(3):
            for i in range(3):
                if a == 1:
                    lhs = odd[pl.ds(i, rows)]
                else:
                    lhs = even[pl.ds(i, rows), pl.ds(a * cols, size)]
                part = jnp.dot(
                    lhs.reshape(rows * size, 3 * chans), weights[a * 3 + i], preferred_element_type=f32
                )
                if a + i == 0:
                    acc[...] = part
                else:
                    acc[...] += part

    one, two = phases
    clear(one)
    clear(two)
    for i in (1, 2):
        loads[i].wait()
    count = placed[0][0]
    live = t_of < count
    cnt_own[...] = jnp.full(cnt_own.shape, count.astype(f32), f32)

    for y in range(rows):
        keep(one, y, silu_norm(feat[:, y].astype(f32), g1[...].reshape(1, 1, chans)))

    keep_tail(one)
    pl.semaphore_wait(barrier, expected)
    send(one, True)
    gather(one, True)
    loads[3].wait()
    conv(w1)
    for i in (4, 5, 7):
        loads[i].wait()

    for y in range(rows):
        at = y * frames * cols
        hidden = acc[pl.ds(at, frames * cols)] + b1[...]
        keep(two, y, silu_norm(hidden.reshape(frames, cols, chans), g2[...].reshape(1, 1, chans)))

    keep_tail(two)
    send(two, False)
    gather(two, False)
    loads[6].wait()
    conv(w2)

    for y in range(rows):
        at = y * frames * cols
        result = (acc[pl.ds(at, frames * cols)] + b2[...]).reshape(frames, cols, chans)
        result = feat[:, y].astype(f32) + result
        out[:, y] = jnp.where(live, result, 0.0).astype(bf16)

    finish_sends(one, True)
    finish_sends(two, False)


def shards(sizes, features, frame_counts, gain_first, conv_first, bias_first, gain_second, conv_second, bias_second):
    frames, rows, cols, chans = features.shape
    n_t = sizes[0]
    dma = pltpu.SemaphoreType.DMA
    phase = [
        pltpu.VMEM((rows, frames + 2, cols, chans), bf16),
        pltpu.VMEM((2, rows, frames, chans), bf16),
        pltpu.VMEM((rows, 2, cols, chans), bf16),
        pltpu.VMEM((2, 2, rows, chans), bf16),
        pltpu.VMEM((2, frames, cols, chans), bf16),
        pltpu.VMEM((2, rows + 2, frames, chans), bf16),
        pltpu.VMEM((n_t, rows + 2, 2, cols, chans), bf16),
        pltpu.VMEM((n_t, 2, 3, 2, rows, chans), bf16),
        dma((len(DIRS),)),
        dma((len(DIRS),)),
        dma((n_t, len(DIRS))),
        dma((n_t, len(DIRS))),
    ]
    scratch = [
        pltpu.SMEM((1,), jnp.int32),
        pltpu.VMEM(features.shape, bf16),
        pltpu.VMEM((1, chans), f32),
        pltpu.VMEM((9, 3 * chans, chans), bf16),
        pltpu.VMEM((1, chans), f32),
        pltpu.VMEM((1, chans), f32),
        pltpu.VMEM((9, 3 * chans, chans), bf16),
        pltpu.VMEM((1, chans), f32),
        dma((8,)),
        pltpu.VMEM((rows + 2, (frames + 2) * cols, 3 * chans), bf16),
        pltpu.VMEM((rows + 2, frames * cols, 3 * chans), bf16),
        pltpu.VMEM((rows * frames * cols, chans), f32),
        pltpu.VMEM((cols, chans), f32),
        pltpu.VMEM((n_t, cols, chans), f32),
        pltpu.VMEM((rows + 2, 2, cols, chans), f32),
        pltpu.VMEM((2, 3, 2, rows, chans), f32),
        dma((n_t,)),
        dma((n_t,)),
    ]
    vmem = pl.BlockSpec(memory_space=pltpu.VMEM)
    return pl.pallas_call(
        functools.partial(kernel, sizes),
        out_shape=jax.ShapeDtypeStruct(features.shape, features.dtype),
        in_specs=[pl.BlockSpec(memory_space=pltpu.SMEM)] + [pl.BlockSpec(memory_space=pltpu.HBM)] * 7,
        out_specs=vmem,
        scratch_shapes=scratch + phase + phase,
        compiler_params=pltpu.CompilerParams(
            collective_id=0, has_side_effects=True, vmem_limit_bytes=60 << 20
        ),
    )(
        frame_counts,
        features,
        gain_first.reshape(1, chans),
        conv_first.reshape(9, 3 * chans, chans),
        bias_first.reshape(1, chans),
        gain_second.reshape(1, chans),
        conv_second.reshape(9, 3 * chans, chans),
        bias_second.reshape(1, chans),
    )


def solution(mesh):
    sizes = (mesh.shape["tchunk"], mesh.shape["ha"], mesh.shape["wa"])
    spec = P(("grp", "tchunk"), "ha", "wa", None)
    return jax.shard_map(
        functools.partial(shards, sizes),
        mesh=mesh,
        in_specs=(spec, P(("grp", "tchunk")), P(), P(), P(), P(), P(), P()),
        out_specs=spec,
        check_vma=False,
    )
```

time: 78 us -> 21.8 us (0.28)
  Pallas kernels: 0 us -> 19.4 us
  matrix products: 17.9 us -> 0 us
  blocking collectives: 15.7 us -> 0 us
  starting transfers between devices: 15.4 us -> 0 us
  waiting for transfers between devices: 12.8 us -> 0 us
  other arithmetic: 9.52 us -> 0 us
  loops' own time: 2.76 us -> 0 us
    pallas_call x0 -> x1, Pallas kernels: none -> 19.4 us  [shards(): pl.pallas_call(functools.partial(kernel, sizes), out_shape=jax.ShapeDtype...]
    conv_general_dilated x2 -> x0, matrix products: 17.9 us -> none  [causal_conv(): lax.conv_general_dilated(stacked[None], kernel, (1, 1, 1), 'VALID', dimen...]
    ppermute x8 -> x0, starting transfers between devices: 15.4 us -> none  [the longest x4 10.1 us: extended(): lax.ppermute(lax.slice_in_dim(block, block.shape[dim] - width, None, axis...]
    ppermute x8 -> x0, waiting for transfers between devices: 12.8 us -> none  [the longest x4 12.1 us: extended(): lax.ppermute(lax.slice_in_dim(block, 0, width, axis=dim), axis, backward)]
    all_gather x2 -> x0, blocking collectives: 10.8 us -> none  [prefix(): everything = jax.tree.map(lambda part: lax.all_gather(part, axis), value)]
    unnamed x1 -> x0, blocking collectives: 4.92 us -> none
    select_n x6 -> x0, other arithmetic: 3.82 us -> none  [the longest x4 2.38 us: turn(): return jax.tree.map(lambda a, b: jnp.where(reached, a, b), new, before)]
    another operation x2 -> x0, loops' own time: 2.76 us -> none  [prefix(): return lax.fori_loop(0, devices, turn, start)]
  transfers between devices with their start and end apart: 8 -> 0, of which waited for: 6 -> 0; matrix products, arithmetic and copies ran while one was open for 0% -> 0% of each run, Pallas kernels for 0% -> 0%
where the time goes in v1:
time: 21.8 us; the launch traced here: 21.7 us
  Pallas kernels  19.4 us (89%)
  local copies, waits for them, and re-layouts  1.67 us (8%)
  between operations  0.66 us (3%)
    pallas_call x1, Pallas kernels, shards(): pl.pallas_call(functools.partial(kernel, sizes), out_shape=jax.ShapeDtype...  19.4 us
    unnamed x1, local copies, waits for them, and re-layouts  1.67 us

profile of v1, /device:TPU:0, one launch (start us, length us, event | category | flops | bytes accessed | tf_op | source)
XLA Modules:
  0.0 21.7 jit_solution(9458873011356832461)
XLA Ops:
  0.7 19.4 %shard_map.82 = bf16[8,8,8,192]{3,2,1,0:T(8,128)(2,1)} custom-call(s32[1]{0:T(128)S(6)} %copy.10.refs_0_, bf16[8,8,8,192]{3,2,1,0:T(8,128)(2,1)} %refs_1_.1, f32[1,192]{1,0:T(1,128)} %bitcast.8, bf16[9,576,192]{2,1,0:T(8,128)(2,1)} %bitcast.6, f32[1,192]{1,0:T(1,128)} %bitcast.9, f32[1,192]{1,0:T(1,128)} %bitcast.10, bf16[9,576,192]{2,1,0:T(8,128)(2,1)} %bitcast.7, ...), custom_call_target="tpu_custom_call" | custom-call | tf_op jit(solution)/shard_map/pallas_call | solution.py:335
  20.0 1.7 %copy.11 = bf16[8,8,8,192]{3,2,1,0:T(8,128)(2,1)} copy(bf16[8,8,8,192]{3,2,1,0:T(8,128)(2,1)} %shard_map.82) | data formatting | bytes 393216
